TPU v7x, 128 devices: a whole 4x4x4 slice. The times are simulated.
128 devices in a mesh: rep: 16 (over y, z), tp: 8 (over x, core).
Axes of the slice: x: 4, y: 4, z: 4, core: 2. Of those that a mesh axis runs over, the one named last changes fastest.
Arguments:
- grads: bfloat16 [16, 12, 768, 2048], P('rep', None, None, 'tp'), may hold values from -6 to 6
- error: float32 [16, 12, 768, 2048], P('rep', None, None, 'tp'), may hold values from -2 to 2
- query: float32 [12, 32, 2048], P(None, None, 'tp'), may hold values from -6 to 6
- momentum: float32 [9216, 2048], P(('rep', 'tp')), may hold values from -0.8 to 0.8
- master: float32 [9216, 2048], P(('rep', 'tp')), may hold values from -0.8 to 0.8
Outputs:
- new_error: float32 [16, 12, 768, 2048], P('rep', None, None, 'tp')
- new_query: float32 [12, 32, 2048], P(None, None, 'tp')
- new_momentum: float32 [9216, 2048], P(('rep', 'tp'))
- new_master: float32 [9216, 2048], P(('rep', 'tp'))
- weights: bfloat16 [12, 768, 2048], P(None, None, 'tp')
All inputs are finite; a program needn't handle non-finite values.
Results may differ from a plain program's by a relative error of at most 0.0004.
Values may be sent and summed in bfloat16 or wider, within the bound.
A program may use at most 128 MiB of HBM per device.

v0:
```python
import jax
import jax.numpy as jnp
from jax import lax
from jax.sharding import PartitionSpec as P

ROUNDS = 2
NS_STEPS = 5
NORM_EPSILON = 1e-06
MOMENTUM_DECAY = 0.9
LEARNING_RATE = 0.5


def local_gram(factor):
    return jnp.einsum("krd,ksd->krs", factor, factor, precision=lax.Precision.HIGHEST)


def orthonormal(factor, gram_of):
    gram_now = gram_of(factor)
    sum_squares = jnp.trace(gram_now, axis1=1, axis2=2)[:, None, None]
    factor_scale = lax.rsqrt(sum_squares + NORM_EPSILON)
    ortho_basis = factor * factor_scale
    gram_now = gram_now * (factor_scale * factor_scale)
    for iteration in range(NS_STEPS):
        if iteration > 0:
            gram_now = gram_of(ortho_basis)
        ortho_basis = 1.5 * ortho_basis - 0.5 * jnp.einsum(
            "krs,ksd->krd", gram_now, ortho_basis, precision=lax.Precision.HIGHEST
        )
    return ortho_basis


def local(grads, error, query, momentum, master):
    corrected = grads[0].astype(jnp.float32) + error[0]
    current = query
    replicas = lax.axis_size("rep")
    for power_pass in range(ROUNDS):
        partial_factor = jnp.einsum(
            "kdf,krf->krd", corrected, current, precision=lax.Precision.HIGHEST
        )
        summed = lax.psum(partial_factor, ("rep", "tp"))
        ortho_basis = orthonormal(summed, local_gram)
        partial_query = jnp.einsum(
            "kdf,krd->krf", corrected, ortho_basis, precision=lax.Precision.HIGHEST
        )
        current = lax.psum(partial_query, "rep") / replicas
    approx = jnp.einsum("krd,krf->kdf", ortho_basis, current, precision=lax.Precision.HIGHEST)
    new_error = (corrected - approx)[None]
    matrices, model_width, shard_cols = approx.shape
    block_rows = matrices * model_width // replicas
    approx_rows = approx.reshape(matrices * model_width, shard_cols)
    own_block = lax.dynamic_slice_in_dim(
        approx_rows, lax.axis_index("rep") * block_rows, block_rows, 0
    )
    flat_approx = lax.all_to_all(own_block, "tp", split_axis=0, concat_axis=1, tiled=True)
    new_momentum = MOMENTUM_DECAY * momentum + flat_approx
    new_master = master - LEARNING_RATE * new_momentum
    working = new_master.astype(jnp.bfloat16)
    by_columns = lax.all_to_all(working, "tp", split_axis=1, concat_axis=0, tiled=True)
    weight_rows = lax.all_gather(by_columns, "rep", axis=0, tiled=True)
    weights = weight_rows.reshape(matrices, model_width, shard_cols)
    return (new_error, current, new_momentum, new_master, weights)


def solution(mesh):
    placed = (
        P("rep", None, None, "tp"),
        P("rep", None, None, "tp"),
        P(None, None, "tp"),
        P(("rep", "tp"), None),
        P(("rep", "tp"), None),
    )
    return jax.shard_map(
        local,
        mesh=mesh,
        in_specs=placed,
        out_specs=(
            P("rep", None, None, "tp"),
            P(None, None, "tp"),
            P(("rep", "tp"), None),
            P(("rep", "tp"), None),
            P(None, None, "tp"),
        ),
        check_vma=False,
    )
```

profile of v0, /device:TPU:1, one launch (start us, length us, event | category | flops | bytes accessed | tf_op | source)
XLA Modules:
  0.0 643.5 jit_solution(3805032442626660912)
XLA Ops:
  8.2 14.9 %fusion.9 = f32[12,32,768]{2,1,0:T(8,128)} fusion(f32[12,32,256]{2,1,0:T(8,128)S(1)} %copy-done, f32[1,12,768,256]{3,2,1,0:T(8,128)} %param.6, bf16[1,12,768,256]{3,2,1,0:T(8,128)(2,1)} %param.5), kind=kOutput, calls=%fused_computation.11 | convolution fusion | flops 910688256 | bytes 15728640 | tf_op jit(solution)/shard_map/kdf,krf->krd/dot_general | solution.py:37
  23.3 150.7 %all-reduce.5.cloned.1.call-done = f32[12,32,768]{2,1,0:T(8,128)} async-done(((f32[12,32,768]{2,1,0:T(8,128)}), f32[12,32,768]{2,1,0:T(8,128)}) %all-reduce.5.cloned.1.call-update) | async-done | bytes 1179664 | tf_op jit(solution)/shard_map/psum | solution.py:40
  174.1 3.0 select_reduce_fusion.1
  177.1 1.3 fusion.21
  178.4 1.2 fusion.36
  179.6 1.2 fusion.20
  180.9 1.2 fusion.37
  183.3 1.2 fusion.38
  185.7 1.2 fusion.39
  186.9 1.2 fusion.17
  188.6 6.7 %fusion.4 = f32[12,32,256]{2,1,0:T(8,128)} fusion(f32[12,32,768]{2,1,0:T(8,128)S(1)} %fusion.17, f32[1,12,768,256]{3,2,1,0:T(8,128)S(1)} %bitcast.73, bf16[1,12,768,256]{3,2,1,0:T(8,128)(2,1)S(1)} %bitcast.77), kind=kOutput, calls=%fused_computation.5 | convolution fusion | flops 910688256 | bytes 15728640 | tf_op jit(solution)/shard_map/kdf,krd->krf/dot_general | solution.py:42
  195.4 81.4 %all-reduce.7.cloned.1.call-done = f32[12,32,256]{2,1,0:T(8,128)} async-done(((f32[12,32,256]{2,1,0:T(8,128)}), f32[12,32,256]{2,1,0:T(8,128)}) %all-reduce.7.cloned.1.call-update) | async-done | bytes 393232 | tf_op jit(solution)/shard_map/psum | solution.py:45
  276.8 14.6 %fusion.2 = f32[12,32,768]{2,1,0:T(8,128)} fusion(f32[12,32,256]{2,1,0:T(8,128)} %all-reduce.7.cloned.1.call-done, f32[1,12,768,256]{3,2,1,0:T(8,128)} %param.6, bf16[1,12,768,256]{3,2,1,0:T(8,128)(2,1)} %param.5), kind=kOutput, calls=%fused_computation.3 | convolution fusion | flops 910786560 | bytes 15728640 | tf_op jit(solution)/shard_map/kdf,krf->krd/dot_general | solution.py:37
  291.6 148.1 %all-reduce.9.cloned.1.call-done = f32[12,32,768]{2,1,0:T(8,128)} async-done(((f32[12,32,768]{2,1,0:T(8,128)}), f32[12,32,768]{2,1,0:T(8,128)}) %all-reduce.9.cloned.1.call-update) | async-done | bytes 1179664 | tf_op jit(solution)/shard_map/psum | solution.py:40
  439.7 3.0 select_reduce_fusion
  442.7 1.3 fusion.16
  444.0 1.2 fusion.40
  445.3 1.2 fusion.15
  446.5 1.2 fusion.41
  447.7 1.2 fusion.14
  448.9 1.2 fusion.42
  450.1 1.2 fusion.13
  451.3 1.2 fusion.43
  454.0 6.8 %fusion = f32[12,32,256]{2,1,0:T(8,128)} fusion(f32[12,32,768]{2,1,0:T(8,128)S(1)} %fusion.12, f32[1,12,768,256]{3,2,1,0:T(8,128)S(1)} %bitcast.75, bf16[1,12,768,256]{3,2,1,0:T(8,128)(2,1)S(1)} %bitcast.79), kind=kOutput, calls=%fused_computation.1 | convolution fusion | flops 910688256 | bytes 15728640 | tf_op jit(solution)/shard_map/kdf,krd->krf/dot_general | solution.py:42
  460.8 81.4 %all-reduce.11.cloned.1.call-done = f32[12,32,256]{2,1,0:T(8,128)} async-done(((f32[12,32,256]{2,1,0:T(8,128)}), f32[12,32,256]{2,1,0:T(8,128)}) %all-reduce.11.cloned.1.call-update) | async-done | bytes 393232 | tf_op jit(solution)/shard_map/psum | solution.py:45
  543.3 7.7 %fusion.44 = f32[12,768,256]{2,1,0:T(8,128)S(1)} fusion(f32[12,32,768]{2,1,0:T(8,128)S(1)} %fusion.12, f32[12,32,256]{2,1,0:T(8,128)S(1)} %broadcast_multiply_fusion), kind=kOutput, calls=%fused_computation.64 | convolution fusion | flops 905969664 | bytes 11010048 | tf_op jit(solution)/shard_map/krd,krf->kdf/dot_general | solution.py:46
  551.1 16.7 %all_to_all.38 = f32[8,72,256]{2,1,0:T(8,128)S(1)} all-to-all(f32[8,72,256]{2,1,0:T(8,128)S(1)} %bitcast.83), channel_id=1, replica_groups=mesh['rep'=16,'tp'=8] {'tp'}, dimensions={0} | all-to-all | bytes 1179648 | tf_op jit(solution)/shard_map/all_to_all | solution.py:54
  567.9 1.2 fusion.35
  569.1 11.1 %all_to_all.39 = bf16[72,8,256]{2,0,1:T(8,128)(2,1)} all-to-all(bf16[72,8,256]{2,0,1:T(8,128)(2,1)S(1)} %bitcast.87), channel_id=1, replica_groups=mesh['rep'=16,'tp'=8] {'tp'}, dimensions={1} | all-to-all | bytes 589824 | tf_op jit(solution)/shard_map/all_to_all | solution.py:58
  580.3 12.7 %fusion.8 = f32[1,12,768,256]{3,2,1,0:T(8,128)} fusion(f32[12,768,256]{2,1,0:T(8,128)} %copy-done.2, f32[1,12,768,256]{3,2,1,0:T(8,128)} %param.6, bf16[1,12,768,256]{3,2,1,0:T(8,128)(2,1)} %param.5), kind=kLoop, calls=%fused_computation.9 | loop fusion | flops 7077888 | bytes 33030144 | tf_op jit(solution)/shard_map/broadcast_in_dim | solution.py:47
  592.9 38.9 %all-gather.2.cloned.1.call-done = bf16[9216,256]{1,0:T(8,128)(2,1)} async-done(((bf16[576,256]{1,0:T(8,128)(2,1)}), bf16[9216,256]{1,0:T(8,128)(2,1)}) %all-gather.2.cloned.1.call-update) | async-done | bytes 4718608 | tf_op jit(solution)/shard_map/all_gather | solution.py:59
  631.8 4.9 copy.24
  (60 shorter events, 6.8 us)
Async XLA Ops:
  7.2 1.0 copy-start
  7.2 166.9 %all-reduce.5.cloned.1.call-start = ((), (), s32[]{:S(2)}) async-start(), calls=%async_computation.2 | async-start | bytes 2359296 | tf_op jit(solution)/shard_map/psum | solution.py:40
  23.1 253.7 %all-reduce.7.cloned.1.call-start = ((), (), s32[]{:S(2)}) async-start(), calls=%async_computation.3 | async-start | bytes 786432 | tf_op jit(solution)/shard_map/psum | solution.py:45
  174.1 3.0 copy-start.3
  178.4 9.7 %slice-start = ((s8[9437184]{0:T(1024)(128)(4,1)}), s8[4194304]{0:T(1024)(128)(4,1)S(1)}, s32[]{:S(2)}) async-start(s8[9437184]{0:T(1024)(128)(4,1)} %bitcast.72), calls=%async_computation.7 | async-start | bytes 8388608
  179.6 8.9 %slice-start.6 = ((s8[4718592]{0:T(1024)(128)(4,1)}), s8[4194304]{0:T(1024)(128)(4,1)S(1)}, s32[]{:S(2)}) async-start(s8[4718592]{0:T(1024)(128)(4,1)} %bitcast.76), calls=%async_computation.13 | async-start | bytes 8388608
  180.9 7.6 %slice-start.1 = ((s8[9437184]{0:T(1024)(128)(4,1)}), s8[4194304]{0:T(1024)(128)(4,1)S(1)}, s32[]{:S(2)}) async-start(s8[9437184]{0:T(1024)(128)(4,1)} %bitcast.72), calls=%async_computation.8 | async-start | bytes 8388608
  183.3 5.3 slice-start.7
  184.5 4.0 slice-start.2
  195.3 244.4 %all-reduce.9.cloned.1.call-start = ((), (), s32[]{:S(2)}) async-start(), calls=%async_computation.4 | async-start | bytes 2359296 | tf_op jit(solution)/shard_map/psum | solution.py:40
  291.4 250.9 %all-reduce.11.cloned.1.call-start = ((), (), s32[]{:S(2)}) async-start(), calls=%async_computation.5 | async-start | bytes 786432 | tf_op jit(solution)/shard_map/psum | solution.py:45
  439.7 3.0 copy-start.4
  444.0 9.7 %slice-start.3 = ((s8[9437184]{0:T(1024)(128)(4,1)}), s8[4194304]{0:T(1024)(128)(4,1)S(1)}, s32[]{:S(2)}) async-start(s8[9437184]{0:T(1024)(128)(4,1)} %bitcast.74), calls=%async_computation.10 | async-start | bytes 8388608
  445.2 8.5 %slice-start.8 = ((s8[4718592]{0:T(1024)(128)(4,1)}), s8[4194304]{0:T(1024)(128)(4,1)S(1)}, s32[]{:S(2)}) async-start(s8[4718592]{0:T(1024)(128)(4,1)} %bitcast.78), calls=%async_computation.15 | async-start | bytes 8388608
  446.5 7.2 %slice-start.4 = ((s8[9437184]{0:T(1024)(128)(4,1)}), s8[4194304]{0:T(1024)(128)(4,1)S(1)}, s32[]{:S(2)}) async-start(s8[9437184]{0:T(1024)(128)(4,1)} %bitcast.74), calls=%async_computation.11 | async-start | bytes 8388608
  448.9 4.8 slice-start.9
  450.1 3.8 slice-start.5
  460.8 171.1 %all-gather.2.cloned.1.call-start = ((), (), s32[]{:S(2)}) async-start(), calls=%async_computation.6 | async-start | bytes 5013504 | tf_op jit(solution)/shard_map/all_gather | solution.py:59
  543.3 7.8 %copy-start.5 = (f32[12,32,256]{2,1,0:T(8,128)}, f32[12,32,256]{2,1,0:T(8,128)S(1)}, u32[]{:S(2)}) copy-start(f32[12,32,256]{2,1,0:T(8,128)S(1)} %broadcast_multiply_fusion) | copy-start | bytes 1179652
  551.0 18.1 %copy-start.2 = (f32[12,768,256]{2,1,0:T(8,128)}, f32[12,768,256]{2,1,0:T(8,128)S(1)}, u32[]{:S(2)}) copy-start(f32[12,768,256]{2,1,0:T(8,128)S(1)} %fusion.44) | copy-start | bytes 28311556
  551.1 16.8 %copy-start.6 = (f32[72,2048]{1,0:T(8,128)S(1)}, f32[72,2048]{1,0:T(8,128)}, u32[]{:S(2)}) copy-start(f32[72,2048]{1,0:T(8,128)} %param.9) | copy-start | bytes 1769476
  551.1 16.8 %copy-start.7 = (f32[72,2048]{1,0:T(8,128)S(1)}, f32[72,2048]{1,0:T(8,128)}, u32[]{:S(2)}) copy-start(f32[72,2048]{1,0:T(8,128)} %param.8) | copy-start | bytes 1769476
  631.8 4.9 copy-start.1
Sparse Core Ops, SparseCore 0:
  23.2 150.8 all-reduce.4
  195.4 81.3 all-reduce.6
  291.5 148.1 all-reduce.8
  460.9 81.3 all-reduce.10
  580.4 51.3 all-gather.1
where the time goes:
time: 649 us; the launch traced here: 643 us
  waiting for transfers between devices  501 us (77%)
  matrix products  78.5 us (12%)
  blocking collectives  27.8 us (4%)
  other arithmetic  14.9 us (2%)
  between operations  14.6 us (2%)
    psum x2, waiting for transfers between devices, local(): summed = lax.psum(partial_factor, ('rep', 'tp'))  299 us
    psum x2, waiting for transfers between devices, local(): current = lax.psum(partial_query, 'rep') / replicas  163 us
    all_gather x1, waiting for transfers between devices, local(): weight_rows = lax.all_gather(by_columns, 'rep', axis=0, tiled=True)  38.9 us
    dot_general x2, matrix products, local(): jnp.einsum('kdf,krf->krd', corrected, current, precision=lax.Precision.HI...  29.5 us
    all_to_all x1, blocking collectives, local(): lax.all_to_all(own_block, 'tp', split_axis=0, concat_axis=1, tiled=True)  16.7 us
    dot_general x10, matrix products, local_gram(): jnp.einsum('krd,ksd->krs', factor, factor, precision=lax.Precision.HIGHEST)  15.7 us
    dot_general x2, matrix products, local(): jnp.einsum('kdf,krd->krf', corrected, ortho_basis, precision=lax.Precisio...  13.5 us
  transfers between devices with their start and end apart: 5, of which 5 were waited for; matrix products, arithmetic and copies ran while one was open for 2% of the time, Pallas kernels for 0%

commit v1 on v0

--- a/solution.py
+++ b/solution.py
@@ -8,6 +8,27 @@
 NORM_EPSILON = 1e-06
 MOMENTUM_DECAY = 0.9
 LEARNING_RATE = 0.5
+
+
+def collect(x, axis, dim):
+    devices, index, rows = (lax.axis_size(axis), lax.axis_index(axis), x.shape[dim])
+    right = [(i, (i + 1) % devices) for i in range(devices)]
+    left = [(i, (i - 1) % devices) for i in range(devices)]
+    out = jnp.zeros((*x.shape[:dim], devices * rows, *x.shape[dim + 1 :]), x.dtype)
+    out = lax.dynamic_update_slice_in_dim(out, x, index * rows, axis=dim)
+    from_left = from_right = x
+    half = devices // 2
+    for lap in range(1, half + 1):
+        from_left = lax.ppermute(from_left, axis, right)
+        out = lax.dynamic_update_slice_in_dim(
+            out, from_left, (index - lap) % devices * rows, axis=dim
+        )
+        if lap < devices - half:
+            from_right = lax.ppermute(from_right, axis, left)
+            out = lax.dynamic_update_slice_in_dim(
+                out, from_right, (index + lap) % devices * rows, axis=dim
+            )
+    return out
 
 
 def local_gram(factor):
@@ -56,7 +77,7 @@
     new_master = master - LEARNING_RATE * new_momentum
     working = new_master.astype(jnp.bfloat16)
     by_columns = lax.all_to_all(working, "tp", split_axis=1, concat_axis=0, tiled=True)
-    weight_rows = lax.all_gather(by_columns, "rep", axis=0, tiled=True)
+    weight_rows = collect(by_columns, "rep", 0)
     weights = weight_rows.reshape(matrices, model_width, shard_cols)
     return (new_error, current, new_momentum, new_master, weights)
 

time: 649 us -> 687 us (1.059); the launches traced: 643 us -> 674 us
  starting transfers between devices: 0.56 us -> 35.4 us
    all_gather x1 -> x0, waiting for transfers between devices: 38.9 us -> none  [local(): weight_rows = lax.all_gather(by_columns, 'rep', axis=0, tiled=True)]
    ppermute x0 -> x15, waiting for transfers between devices: none -> 36.4 us  [the longest x8 36.2 us: collect(): from_left = lax.ppermute(from_left, axis, right)]
    ppermute x0 -> x15, starting transfers between devices: none -> 34.8 us  [the longest x7 34 us: collect(): from_right = lax.ppermute(from_right, axis, left)]
  transfers between devices with their start and end apart: 5 -> 19, of which waited for: 5 -> 12; matrix products, arithmetic and copies ran while one was open for 2% -> 2% of each run, Pallas kernels for 0% -> 0%
where the time goes in v1:
time: 687 us; the launch traced here: 674 us
  waiting for transfers between devices  498 us (72%)
  matrix products  78.9 us (11%)
  starting transfers between devices  35.4 us (5%)
  blocking collectives  27.1 us (4%)
  between operations  15 us (2%)
  other arithmetic  14.7 us (2%)
    psum x2, waiting for transfers between devices, local(): summed = lax.psum(partial_factor, ('rep', 'tp'))  299 us
    psum x2, waiting for transfers between devices, local(): current = lax.psum(partial_query, 'rep') / replicas  163 us
    ppermute x8, waiting for transfers between devices, collect(): from_left = lax.ppermute(from_left, axis, right)  36.2 us
    ppermute x7, starting transfers between devices, collect(): from_right = lax.ppermute(from_right, axis, left)  34 us
    dot_general x2, matrix products, local(): jnp.einsum('kdf,krf->krd', corrected, current, precision=lax.Precision.HI...  29.5 us
    all_to_all x1, blocking collectives, local(): lax.all_to_all(own_block, 'tp', split_axis=0, concat_axis=1, tiled=True)  16.7 us
    dot_general x10, matrix products, local_gram(): jnp.einsum('krd,ksd->krs', factor, factor, precision=lax.Precision.HIGHEST)  15.8 us
  transfers between devices with their start and end apart: 19, of which 12 were waited for; matrix products, arithmetic and copies ran while one was open for 2% of the time, Pallas kernels for 0%

profile of v1, /device:TPU:1, one launch (start us, length us, event | category | flops | bytes accessed | tf_op | source)
XLA Modules:
  0.0 673.9 jit_solution(306003683424765598)
XLA Ops:
  8.2 14.9 %fusion.9 = f32[12,32,768]{2,1,0:T(8,128)} fusion(f32[12,32,256]{2,1,0:T(8,128)S(1)} %copy-done, f32[1,12,768,256]{3,2,1,0:T(8,128)} %param.6, bf16[1,12,768,256]{3,2,1,0:T(8,128)(2,1)} %param.5), kind=kOutput, calls=%fused_computation.11 | convolution fusion | flops 910688256 | bytes 15728640 | tf_op jit(solution)/shard_map/kdf,krf->krd/dot_general | solution.py:58
  23.4 150.7 %all-reduce.5.cloned.1.call-done = f32[12,32,768]{2,1,0:T(8,128)} async-done(((f32[12,32,768]{2,1,0:T(8,128)}), f32[12,32,768]{2,1,0:T(8,128)}) %all-reduce.5.cloned.1.call-update) | async-done | bytes 1179664 | tf_op jit(solution)/shard_map/psum | solution.py:61
  174.1 3.1 select_reduce_fusion.1
  177.2 1.3 fusion.21
  188.7 6.7 fusion.4
  195.5 81.4 %all-reduce.7.cloned.1.call-done = f32[12,32,256]{2,1,0:T(8,128)} async-done(((f32[12,32,256]{2,1,0:T(8,128)}), f32[12,32,256]{2,1,0:T(8,128)}) %all-reduce.7.cloned.1.call-update) | async-done | bytes 393232 | tf_op jit(solution)/shard_map/psum | solution.py:66
  276.9 14.6 %fusion.2 = f32[12,32,768]{2,1,0:T(8,128)} fusion(f32[12,32,256]{2,1,0:T(8,128)} %all-reduce.7.cloned.1.call-done, f32[1,12,768,256]{3,2,1,0:T(8,128)} %param.6, bf16[1,12,768,256]{3,2,1,0:T(8,128)(2,1)} %param.5), kind=kOutput, calls=%fused_computation.3 | convolution fusion | flops 910786560 | bytes 15728640 | tf_op jit(solution)/shard_map/kdf,krf->krd/dot_general | solution.py:58
  291.8 148.1 %all-reduce.9.cloned.1.call-done = f32[12,32,768]{2,1,0:T(8,128)} async-done(((f32[12,32,768]{2,1,0:T(8,128)}), f32[12,32,768]{2,1,0:T(8,128)}) %all-reduce.9.cloned.1.call-update) | async-done | bytes 1179664 | tf_op jit(solution)/shard_map/psum | solution.py:61
  439.9 3.1 select_reduce_fusion
  443.0 1.3 fusion.16
  445.5 1.2 fusion.15
  454.2 6.8 %fusion = f32[12,32,256]{2,1,0:T(8,128)} fusion(f32[12,32,768]{2,1,0:T(8,128)S(1)} %fusion.12, f32[1,12,768,256]{3,2,1,0:T(8,128)S(1)} %bitcast.75, bf16[1,12,768,256]{3,2,1,0:T(8,128)(2,1)S(1)} %bitcast.79), kind=kOutput, calls=%fused_computation.1 | convolution fusion | flops 910688256 | bytes 15728640 | tf_op jit(solution)/shard_map/kdf,krd->krf/dot_general | solution.py:63
  461.0 81.5 %all-reduce.11.cloned.1.call-done = f32[12,32,256]{2,1,0:T(8,128)} async-done(((f32[12,32,256]{2,1,0:T(8,128)}), f32[12,32,256]{2,1,0:T(8,128)}) %all-reduce.11.cloned.1.call-update) | async-done | bytes 393232 | tf_op jit(solution)/shard_map/psum | solution.py:66
  543.5 8.0 %fusion.44 = f32[12,768,256]{2,1,0:T(8,128)S(1)} fusion(f32[12,32,768]{2,1,0:T(8,128)S(1)} %fusion.12, f32[12,32,256]{2,1,0:T(8,128)S(1)} %broadcast_multiply_fusion), kind=kOutput, calls=%fused_computation.80 | convolution fusion | flops 905969664 | bytes 11010048 | tf_op jit(solution)/shard_map/krd,krf->kdf/dot_general | solution.py:67
  551.7 16.7 %all_to_all.38 = f32[8,72,256]{2,1,0:T(8,128)S(1)} all-to-all(f32[8,72,256]{2,1,0:T(8,128)S(1)} %bitcast.84), channel_id=1, replica_groups=mesh['rep'=16,'tp'=8] {'tp'}, dimensions={0} | all-to-all | bytes 1179648 | tf_op jit(solution)/shard_map/all_to_all | solution.py:75
  569.6 10.4 %all_to_all.39 = bf16[72,8,256]{2,0,1:T(8,128)(2,1)S(1)} all-to-all(bf16[72,8,256]{2,0,1:T(8,128)(2,1)S(1)} %bitcast.86), channel_id=1, replica_groups=mesh['rep'=16,'tp'=8] {'tp'}, dimensions={1} | all-to-all | bytes 589824 | tf_op jit(solution)/shard_map/all_to_all | solution.py:79
  580.9 4.0 collective-permute-start.1
  584.9 6.5 collective-permute-done
  591.4 4.8 collective-permute-start.3
  596.2 5.6 collective-permute-done.2
  601.8 4.8 collective-permute-start.5
  606.6 12.5 %fusion.8 = f32[1,12,768,256]{3,2,1,0:T(8,128)} fusion(f32[12,768,256]{2,1,0:T(8,128)} %copy-done.2, f32[1,12,768,256]{3,2,1,0:T(8,128)} %param.6, bf16[1,12,768,256]{3,2,1,0:T(8,128)(2,1)} %param.5), kind=kLoop, calls=%fused_computation.9 | loop fusion | flops 7077888 | bytes 33030144 | tf_op jit(solution)/shard_map/broadcast_in_dim | solution.py:68
  619.5 4.8 collective-permute-start.7
  624.4 3.6 collective-permute-done.6
  628.1 5.2 collective-permute-start.9
  633.3 3.6 collective-permute-done.8
  637.0 5.2 collective-permute-start.11
  642.2 3.6 collective-permute-done.10
  645.9 5.2 collective-permute-start.13
  651.1 3.6 collective-permute-done.12
  655.0 9.7 %collective-permute-done.14 = bf16[576,256]{1,0:T(8,128)(2,1)S(1)} collective-permute-done((bf16[576,256]{1,0:T(8,128)(2,1)S(1)}, bf16[576,256]{1,0:T(8,128)(2,1)S(1)}, u32[]{:S(2)}, u32[]{:S(2)}) %collective-permute-start.14) | collective-permute-done | bytes 294944 | tf_op jit(solution)/shard_map/ppermute | solution.py:22
  664.7 2.2 copy-done.5
  (105 shorter events, 24.2 us)
Async XLA Ops:
  7.2 166.9 %all-reduce.5.cloned.1.call-start = ((), (), s32[]{:S(2)}) async-start(), calls=%async_computation.2 | async-start | bytes 2359296 | tf_op jit(solution)/shard_map/psum | solution.py:61
  23.1 253.8 %all-reduce.7.cloned.1.call-start = ((), (), s32[]{:S(2)}) async-start(), calls=%async_computation.3 | async-start | bytes 786432 | tf_op jit(solution)/shard_map/psum | solution.py:66
  178.5 9.7 %slice-start = ((s8[9437184]{0:T(1024)(128)(4,1)}), s8[4194304]{0:T(1024)(128)(4,1)S(1)}, s32[]{:S(2)}) async-start(s8[9437184]{0:T(1024)(128)(4,1)} %bitcast.72), calls=%async_computation.6 | async-start | bytes 8388608
  179.7 8.9 %slice-start.6 = ((s8[4718592]{0:T(1024)(128)(4,1)}), s8[4194304]{0:T(1024)(128)(4,1)S(1)}, s32[]{:S(2)}) async-start(s8[4718592]{0:T(1024)(128)(4,1)} %bitcast.76), calls=%async_computation.12 | async-start | bytes 8388608
  181.0 7.7 %slice-start.1 = ((s8[9437184]{0:T(1024)(128)(4,1)}), s8[4194304]{0:T(1024)(128)(4,1)S(1)}, s32[]{:S(2)}) async-start(s8[9437184]{0:T(1024)(128)(4,1)} %bitcast.72), calls=%async_computation.7 | async-start | bytes 8388608
  183.4 5.3 slice-start.7
  195.5 244.4 %all-reduce.9.cloned.1.call-start = ((), (), s32[]{:S(2)}) async-start(), calls=%async_computation.4 | async-start | bytes 2359296 | tf_op jit(solution)/shard_map/psum | solution.py:61
  291.5 251.0 %all-reduce.11.cloned.1.call-start = ((), (), s32[]{:S(2)}) async-start(), calls=%async_computation.5 | async-start | bytes 786432 | tf_op jit(solution)/shard_map/psum | solution.py:66
  444.3 9.7 %slice-start.3 = ((s8[9437184]{0:T(1024)(128)(4,1)}), s8[4194304]{0:T(1024)(128)(4,1)S(1)}, s32[]{:S(2)}) async-start(s8[9437184]{0:T(1024)(128)(4,1)} %bitcast.74), calls=%async_computation.9 | async-start | bytes 8388608
  445.5 8.5 %slice-start.8 = ((s8[4718592]{0:T(1024)(128)(4,1)}), s8[4194304]{0:T(1024)(128)(4,1)S(1)}, s32[]{:S(2)}) async-start(s8[4718592]{0:T(1024)(128)(4,1)} %bitcast.78), calls=%async_computation.14 | async-start | bytes 8388608
  446.7 7.2 %slice-start.4 = ((s8[9437184]{0:T(1024)(128)(4,1)}), s8[4194304]{0:T(1024)(128)(4,1)S(1)}, s32[]{:S(2)}) async-start(s8[9437184]{0:T(1024)(128)(4,1)} %bitcast.74), calls=%async_computation.10 | async-start | bytes 8388608
  449.1 4.8 slice-start.9
  543.5 8.0 %copy-start.6 = (f32[12,32,256]{2,1,0:T(8,128)}, f32[12,32,256]{2,1,0:T(8,128)S(1)}, u32[]{:S(2)}) copy-start(f32[12,32,256]{2,1,0:T(8,128)S(1)} %broadcast_multiply_fusion) | copy-start | bytes 1179652
  551.6 18.1 %copy-start.2 = (f32[12,768,256]{2,1,0:T(8,128)}, f32[12,768,256]{2,1,0:T(8,128)S(1)}, u32[]{:S(2)}) copy-start(f32[12,768,256]{2,1,0:T(8,128)S(1)} %fusion.44) | copy-start | bytes 28311556
  551.6 16.8 %copy-start.7 = (f32[72,2048]{1,0:T(8,128)S(1)}, f32[72,2048]{1,0:T(8,128)}, u32[]{:S(2)}) copy-start(f32[72,2048]{1,0:T(8,128)} %param.9) | copy-start | bytes 1769476
  551.6 16.8 %copy-start.8 = (f32[72,2048]{1,0:T(8,128)S(1)}, f32[72,2048]{1,0:T(8,128)}, u32[]{:S(2)}) copy-start(f32[72,2048]{1,0:T(8,128)} %param.8) | copy-start | bytes 1769476
  580.1 11.3 %collective-permute-start = (bf16[576,256]{1,0:T(8,128)(2,1)S(1)}, bf16[576,256]{1,0:T(8,128)(2,1)S(1)}, u32[]{:S(2)}, u32[]{:S(2)}) collective-permute-start(bf16[576,256]{1,0:T(8,128)(2,1)S(1)} %bitcast.87), channel_id=1, source_target_pairs={{0,8},{8,16},{16,24},{24,32},{32,40},{40,48},{48,56},{56,64},{64,7... | collective-permute-start | bytes 884744 | tf_op jit(solution)/shard_map/ppermute | solution.py:22
  580.9 10.5 %collective-permute-start.1 = (bf16[576,256]{1,0:T(8,128)(2,1)S(1)}, bf16[576,256]{1,0:T(8,128)(2,1)S(1)}, u32[]{:S(2)}, u32[]{:S(2)}) collective-permute-start(bf16[576,256]{1,0:T(8,128)(2,1)S(1)} %bitcast.88), channel_id=1, source_target_pairs={{0,120},{8,0},{16,8},{24,16},{32,24},{40,32},{48,40},{56,48},{64,5... | collective-permute-start | bytes 884744 | tf_op jit(solution)/shard_map/ppermute | solution.py:27
  591.4 10.4 %collective-permute-start.2 = (bf16[576,256]{1,0:T(8,128)(2,1)S(1)}, bf16[576,256]{1,0:T(8,128)(2,1)S(1)}, u32[]{:S(2)}, u32[]{:S(2)}) collective-permute-start(bf16[576,256]{1,0:T(8,128)(2,1)S(1)} %collective-permute-done), channel_id=1, source_target_pairs={{0,8},{8,16},{16,24},{24,32},{32,40},{40,48},{48,56},{56,64},{64,7... | collective-permute-start | bytes 884744 | tf_op jit(solution)/shard_map/ppermute | solution.py:22
  591.4 10.4 %collective-permute-start.3 = (bf16[576,256]{1,0:T(8,128)(2,1)S(1)}, bf16[576,256]{1,0:T(8,128)(2,1)S(1)}, u32[]{:S(2)}, u32[]{:S(2)}) collective-permute-start(bf16[576,256]{1,0:T(8,128)(2,1)S(1)} %collective-permute-done.1), channel_id=1, source_target_pairs={{0,120},{8,0},{16,8},{24,16},{32,24},{40,32},{48,40},{56,48},{64,5... | collective-permute-start | bytes 884744 | tf_op jit(solution)/shard_map/ppermute | solution.py:27
  601.8 17.3 %collective-permute-start.4 = (bf16[576,256]{1,0:T(8,128)(2,1)S(1)}, bf16[576,256]{1,0:T(8,128)(2,1)S(1)}, u32[]{:S(2)}, u32[]{:S(2)}) collective-permute-start(bf16[576,256]{1,0:T(8,128)(2,1)S(1)} %collective-permute-done.2), channel_id=1, source_target_pairs={{0,8},{8,16},{16,24},{24,32},{32,40},{40,48},{48,56},{56,64},{64,7... | collective-permute-start | bytes 884744 | tf_op jit(solution)/shard_map/ppermute | solution.py:22
  601.8 17.7 %collective-permute-start.5 = (bf16[576,256]{1,0:T(8,128)(2,1)S(1)}, bf16[576,256]{1,0:T(8,128)(2,1)S(1)}, u32[]{:S(2)}, u32[]{:S(2)}) collective-permute-start(bf16[576,256]{1,0:T(8,128)(2,1)S(1)} %collective-permute-done.3), channel_id=1, source_target_pairs={{0,120},{8,0},{16,8},{24,16},{32,24},{40,32},{48,40},{56,48},{64,5... | collective-permute-start | bytes 884744 | tf_op jit(solution)/shard_map/ppermute | solution.py:27
  619.1 8.9 %collective-permute-start.6 = (bf16[576,256]{1,0:T(8,128)(2,1)S(1)}, bf16[576,256]{1,0:T(8,128)(2,1)S(1)}, u32[]{:S(2)}, u32[]{:S(2)}) collective-permute-start(bf16[576,256]{1,0:T(8,128)(2,1)S(1)} %collective-permute-done.4), channel_id=1, source_target_pairs={{0,8},{8,16},{16,24},{24,32},{32,40},{40,48},{48,56},{56,64},{64,7... | collective-permute-start | bytes 884744 | tf_op jit(solution)/shard_map/ppermute | solution.py:22
  619.5 8.5 %collective-permute-start.7 = (bf16[576,256]{1,0:T(8,128)(2,1)S(1)}, bf16[576,256]{1,0:T(8,128)(2,1)S(1)}, u32[]{:S(2)}, u32[]{:S(2)}) collective-permute-start(bf16[576,256]{1,0:T(8,128)(2,1)S(1)} %collective-permute-done.5), channel_id=1, source_target_pairs={{0,120},{8,0},{16,8},{24,16},{32,24},{40,32},{48,40},{56,48},{64,5... | collective-permute-start | bytes 884744 | tf_op jit(solution)/shard_map/ppermute | solution.py:27
  628.0 8.9 %collective-permute-start.8 = (bf16[576,256]{1,0:T(8,128)(2,1)S(1)}, bf16[576,256]{1,0:T(8,128)(2,1)S(1)}, u32[]{:S(2)}, u32[]{:S(2)}) collective-permute-start(bf16[576,256]{1,0:T(8,128)(2,1)S(1)} %collective-permute-done.6), channel_id=1, source_target_pairs={{0,8},{8,16},{16,24},{24,32},{32,40},{40,48},{48,56},{56,64},{64,7... | collective-permute-start | bytes 884744 | tf_op jit(solution)/shard_map/ppermute | solution.py:22
  628.1 8.9 %collective-permute-start.9 = (bf16[576,256]{1,0:T(8,128)(2,1)S(1)}, bf16[576,256]{1,0:T(8,128)(2,1)S(1)}, u32[]{:S(2)}, u32[]{:S(2)}) collective-permute-start(bf16[576,256]{1,0:T(8,128)(2,1)S(1)} %collective-permute-done.7), channel_id=1, source_target_pairs={{0,120},{8,0},{16,8},{24,16},{32,24},{40,32},{48,40},{56,48},{64,5... | collective-permute-start | bytes 884744 | tf_op jit(solution)/shard_map/ppermute | solution.py:27
  636.9 8.9 %collective-permute-start.10 = (bf16[576,256]{1,0:T(8,128)(2,1)S(1)}, bf16[576,256]{1,0:T(8,128)(2,1)S(1)}, u32[]{:S(2)}, u32[]{:S(2)}) collective-permute-start(bf16[576,256]{1,0:T(8,128)(2,1)S(1)} %collective-permute-done.8), channel_id=1, source_target_pairs={{0,8},{8,16},{16,24},{24,32},{32,40},{40,48},{48,56},{56,64},{64,7... | collective-permute-start | bytes 884744 | tf_op jit(solution)/shard_map/ppermute | solution.py:22
  637.0 8.9 %collective-permute-start.11 = (bf16[576,256]{1,0:T(8,128)(2,1)S(1)}, bf16[576,256]{1,0:T(8,128)(2,1)S(1)}, u32[]{:S(2)}, u32[]{:S(2)}) collective-permute-start(bf16[576,256]{1,0:T(8,128)(2,1)S(1)} %collective-permute-done.9), channel_id=1, source_target_pairs={{0,120},{8,0},{16,8},{24,16},{32,24},{40,32},{48,40},{56,48},{64,5... | collective-permute-start | bytes 884744 | tf_op jit(solution)/shard_map/ppermute | solution.py:27
  645.8 8.9 %collective-permute-start.12 = (bf16[576,256]{1,0:T(8,128)(2,1)S(1)}, bf16[576,256]{1,0:T(8,128)(2,1)S(1)}, u32[]{:S(2)}, u32[]{:S(2)}) collective-permute-start(bf16[576,256]{1,0:T(8,128)(2,1)S(1)} %collective-permute-done.10), channel_id=1, source_target_pairs={{0,8},{8,16},{16,24},{24,32},{32,40},{40,48},{48,56},{56,64},{64,7... | collective-permute-start | bytes 884744 | tf_op jit(solution)/shard_map/ppermute | solution.py:22
  645.9 9.1 %collective-permute-start.13 = (bf16[576,256]{1,0:T(8,128)(2,1)S(1)}, bf16[576,256]{1,0:T(8,128)(2,1)S(1)}, u32[]{:S(2)}, u32[]{:S(2)}) collective-permute-start(bf16[576,256]{1,0:T(8,128)(2,1)S(1)} %collective-permute-done.11), channel_id=1, source_target_pairs={{0,120},{8,0},{16,8},{24,16},{32,24},{40,32},{48,40},{56,48},{64,5... | collective-permute-start | bytes 884744 | tf_op jit(solution)/shard_map/ppermute | solution.py:27
  651.1 15.8 %copy-start.1 = (f32[12,32,256]{2,1,0:T(8,128)S(1)}, f32[12,32,256]{2,1,0:T(8,128)}, u32[]{:S(2)}) copy-start(f32[12,32,256]{2,1,0:T(8,128)} %param.7) | copy-start | bytes 1179652
  654.7 10.0 %collective-permute-start.14 = (bf16[576,256]{1,0:T(8,128)(2,1)S(1)}, bf16[576,256]{1,0:T(8,128)(2,1)S(1)}, u32[]{:S(2)}, u32[]{:S(2)}) collective-permute-start(bf16[576,256]{1,0:T(8,128)(2,1)S(1)} %collective-permute-done.12), channel_id=1, source_target_pairs={{0,8},{8,16},{16,24},{24,32},{32,40},{40,48},{48,56},{56,64},{64,7... | collective-permute-start | bytes 884744 | tf_op jit(solution)/shard_map/ppermute | solution.py:22
  (6 other events, 17.4 us)
Sparse Core Ops, SparseCore 0:
  23.2 150.8 all-reduce.4
  195.6 81.2 all-reduce.6
  291.7 148.1 all-reduce.8
  461.1 81.3 all-reduce.10
